TPU v7x, 256 devices: a whole 4x4x8 slice. The times are simulated.
256 devices in a mesh: row: 8 (over y, core), col: 32 (over z, x).
Axes of the slice: x: 4, y: 4, z: 8, core: 2. Of those that a mesh axis runs over, the one named last changes fastest.
Arguments:
- diag_block: float32 [1024, 1024], P('row')
- panel: bfloat16 [64, 1024, 1024], P('col', 'row'), may hold values from -1 to 1
- trailing: bfloat16 [32, 12, 1024, 1024], P('col', None, 'row'), may hold values from -6 to 6
- slot_rows: int32 [32, 12], replicated, may hold values from -1 to 63, as said below
- slot_cols: int32 [32, 12], replicated, may hold values from 0 to 1, as said below
Outputs:
- panel_factor: bfloat16 [64, 1024, 1024], P('col', 'row')
- updated: bfloat16 [32, 12, 1024, 1024], P('col', None, 'row')
Inputs may be any that keep to these rules, and one draw needn't show every extreme that they name: Slot s of grid column c holds the tile at tile row slot_rows[c, s] and tile column 2 * c + slot_cols[c, s] of the trailing matrix, or nothing where slot_rows[c, s] is -1. Live slots come first in each column; the pairs of one column are distinct and lie on or below the diagonal (tile row at least tile column). Within one grid column, live slots whose tile rows a and a' have a // 2 == a' // 2 have a == a'. Every column holds at least one live slot, column 0 fills all 12 slots and column 16 holds exactly one. `slot_cols`: 0 in empty slots.
All inputs are finite; a program needn't handle non-finite values.
Results may differ from a plain program's by a relative error of at most 0.0019.
Values may be sent and summed in bfloat16 or wider, within the bound.
No kernel may reach another device: no remote copies, remote signals or barrier semaphores. Data moves between devices by JAX's collectives and lax.ppermute only.
A program may use at most 128 MiB of HBM per device.

v0:
```python
import jax
import jax.numpy as jnp
from jax import lax
from jax.sharding import PartitionSpec as P


def slot_product(slices, left_ids, source_tiles, col_ids, position):
    left_slice = lax.dynamic_index_in_dim(slices, left_ids[position], 0, keepdims=False)
    right_tile = lax.dynamic_index_in_dim(source_tiles, col_ids[position], 0, keepdims=False)
    return lax.dot_general(
        left_slice, right_tile, (((1,), (1,)), ((), ())), preferred_element_type=jnp.float32
    )


def subtract_slot(buffer, position, update):
    previous = lax.dynamic_index_in_dim(buffer, position, 0, keepdims=False).astype(jnp.float32)
    return lax.dynamic_update_index_in_dim(
        buffer, (previous - update).astype(jnp.bfloat16), position, 0
    )


def local(diag_block, panel, trailing, slot_rows, slot_cols):
    diag_full = lax.all_gather(diag_block, "row", axis=0, tiled=True)
    factor = jnp.linalg.cholesky(diag_full)
    tile_count, row_count, tile_width = panel.shape
    stacked = panel.astype(jnp.float32).reshape(tile_count * row_count, tile_width)
    solved = lax.linalg.triangular_solve(factor, stacked.T, left_side=True, lower=True)
    panel_factor = solved.T.reshape(tile_count, row_count, tile_width).astype(jnp.bfloat16)
    whole_tiles = lax.all_gather(panel_factor, "row", axis=1, tiled=True)
    column_index = lax.axis_index("col")
    own_rows = lax.dynamic_index_in_dim(slot_rows, column_index, 0, keepdims=False)
    own_cols = lax.dynamic_index_in_dim(slot_cols, column_index, 0, keepdims=False)
    own_count = jnp.sum((own_rows >= 0).astype(jnp.int32))
    slices = lax.all_gather(panel_factor, "col", axis=0, tiled=True)

    def own_step(position, buffer):
        return subtract_slot(
            buffer, position, slot_product(slices, own_rows, whole_tiles, own_cols, position)
        )

    buffer = lax.fori_loop(0, own_count, own_step, trailing[0])
    return (panel_factor, buffer[None])


def solution(mesh):
    return jax.shard_map(
        local,
        mesh=mesh,
        in_specs=(P("row", None), P("col", "row", None), P("col", None, "row", None), P(), P()),
        out_specs=(P("col", "row", None), P("col", None, "row", None)),
        check_vma=False,
    )
```

profile of v0, /device:TPU:1, one launch (start us, length us, event | category | flops | bytes accessed | tf_op | source)
XLA Modules:
  0.0 681.8 jit_solution(6531067428901336610)
XLA Ops:
  9.6 43.7 %all-gather.4.cloned.1.call-done = f32[1024,1024]{0,1:T(8,128)} async-done(((f32[128,1024]{0,1:T(8,128)}), f32[1024,1024]{0,1:T(8,128)}) %all-gather.4.cloned.1.call-update) | async-done | bytes 4194320 | tf_op jit(solution)/shard_map/all_gather | solution.py:23
  53.3 5.3 copy.18
  58.7 4.4 fusion.18
  65.0 11.7 %cholesky.223 = f32[128,128]{1,0:T(8,128)S(1)} custom-call(f32[128,128]{1,0:T(8,128)S(1)} %cholesky.580), custom_call_target="Cholesky" | custom-call | tf_op jit(solution)/shard_map/jit(cholesky)/cholesky | solution.py:24
  76.8 9.8 %custom-call.62 = f32[1,128,128]{1,2,0:T(8,128)S(1)} custom-call(f32[1,128,128]{2,1,0:T(8,128)S(1)} %get-tuple-element.117), custom_call_target="InvertDiagBlocksLowerTriangular" | custom-call | tf_op jit(solution)/shard_map/jit(cholesky)/cholesky | solution.py:24
  93.0 12.2 %cholesky.244 = f32[128,128]{1,0:T(8,128)S(1)} custom-call(f32[128,128]{1,0:T(8,128)S(1)} %cholesky.584), custom_call_target="Cholesky" | custom-call | tf_op jit(solution)/shard_map/jit(cholesky)/cholesky | solution.py:24
  105.8 9.8 %custom-call.63 = f32[1,128,128]{1,2,0:T(8,128)S(1)} custom-call(f32[1,128,128]{2,1,0:T(8,128)S(1)} %get-tuple-element.114), custom_call_target="InvertDiagBlocksLowerTriangular" | custom-call | tf_op jit(solution)/shard_map/jit(cholesky)/cholesky | solution.py:24
  119.0 11.7 %cholesky.468 = f32[128,128]{1,0:T(8,128)S(1)} custom-call(f32[128,128]{1,0:T(8,128)S(1)} %cholesky.589), custom_call_target="Cholesky" | custom-call | tf_op jit(solution)/shard_map/jit(cholesky)/cholesky | solution.py:24
  132.0 9.8 %custom-call.64 = f32[1,128,128]{1,2,0:T(8,128)S(1)} custom-call(f32[1,128,128]{2,1,0:T(8,128)S(1)} %get-tuple-element.111), custom_call_target="InvertDiagBlocksLowerTriangular" | custom-call | tf_op jit(solution)/shard_map/jit(cholesky)/cholesky | solution.py:24
  145.3 11.8 %cholesky.487 = f32[128,128]{1,0:T(8,128)S(1)} custom-call(f32[128,128]{1,0:T(8,128)S(1)} %cholesky.594), custom_call_target="Cholesky" | custom-call | tf_op jit(solution)/shard_map/jit(cholesky)/cholesky | solution.py:24
  158.5 9.8 %custom-call.65 = f32[1,128,128]{1,2,0:T(8,128)S(1)} custom-call(f32[1,128,128]{2,1,0:T(8,128)S(1)} %get-tuple-element.108), custom_call_target="InvertDiagBlocksLowerTriangular" | custom-call | tf_op jit(solution)/shard_map/jit(cholesky)/cholesky | solution.py:24
  171.7 11.7 %cholesky.506 = f32[128,128]{1,0:T(8,128)S(1)} custom-call(f32[128,128]{1,0:T(8,128)S(1)} %cholesky.599), custom_call_target="Cholesky" | custom-call | tf_op jit(solution)/shard_map/jit(cholesky)/cholesky | solution.py:24
  184.7 10.0 %custom-call.66 = f32[1,128,128]{1,2,0:T(8,128)S(1)} custom-call(f32[1,128,128]{2,1,0:T(8,128)S(1)} %get-tuple-element.105), custom_call_target="InvertDiagBlocksLowerTriangular" | custom-call | tf_op jit(solution)/shard_map/jit(cholesky)/cholesky | solution.py:24
  198.1 11.7 %cholesky.526 = f32[128,128]{1,0:T(8,128)S(1)} custom-call(f32[128,128]{1,0:T(8,128)S(1)} %cholesky.604), custom_call_target="Cholesky" | custom-call | tf_op jit(solution)/shard_map/jit(cholesky)/cholesky | solution.py:24
  211.0 9.8 %custom-call.67 = f32[1,128,128]{1,2,0:T(8,128)S(1)} custom-call(f32[1,128,128]{2,1,0:T(8,128)S(1)} %get-tuple-element.102), custom_call_target="InvertDiagBlocksLowerTriangular" | custom-call | tf_op jit(solution)/shard_map/jit(cholesky)/cholesky | solution.py:24
  223.8 12.1 %cholesky.546 = f32[128,128]{1,0:T(8,128)S(1)} custom-call(f32[128,128]{1,0:T(8,128)S(1)} %cholesky.609), custom_call_target="Cholesky" | custom-call | tf_op jit(solution)/shard_map/jit(cholesky)/cholesky | solution.py:24
  237.2 9.8 %custom-call.68 = f32[1,128,128]{1,2,0:T(8,128)S(1)} custom-call(f32[1,128,128]{2,1,0:T(8,128)S(1)} %get-tuple-element.99), custom_call_target="InvertDiagBlocksLowerTriangular" | custom-call | tf_op jit(solution)/shard_map/jit(cholesky)/cholesky | solution.py:24
  249.7 11.7 %cholesky.564 = f32[128,128]{1,0:T(8,128)S(1)} custom-call(f32[128,128]{1,0:T(8,128)S(1)} %convolution_subtract_fusion.13), custom_call_target="Cholesky" | custom-call | tf_op jit(solution)/shard_map/jit(cholesky)/cholesky | solution.py:24
  268.3 4.8 select_select_fusion
  273.1 23.0 %while.12 = (s32[]{:T(128)}, f32[1024,1024]{1,0:T(8,128)}, s32[8,2]{0,1:T(2,128)S(1)}, f32[8,128,128]{2,1,0:T(8,128)S(1)}, s32[]{:T(128)}) while((s32[]{:T(128)}, f32[1024,1024]{1,0:T(8,128)}, s32[8,2]{0,1:T(2,128)S(1)}, f32[8,128,128]{2,1,0:T(8,128)S(1)}, s32[]{:T(128)}) %tuple.74), condition=%wide.while_cond, body=%wide.while_body.sunk | while | flops 2 | bytes 131189 | solution.py:27
  296.1 78.8 %custom-call.69 = f32[8,128,128]{1,2,0:T(8,128)S(1)} custom-call(f32[8,128,128]{2,1,0:T(8,128)S(1)} %get-tuple-element.48), custom_call_target="InvertDiagBlocksLowerTriangular" | custom-call | tf_op jit(solution)/shard_map/triangular_solve | solution.py:27
  398.6 34.2 %all-gather.8.cloned.1.call-done = bf16[2,1024,1024]{2,1,0:T(8,128)(2,1)} async-done(((bf16[2,128,1024]{2,1,0:T(8,128)(2,1)}), bf16[2,1024,1024]{2,1,0:T(8,128)(2,1)}) %all-gather.8.cloned.1.call-update) | async-done | bytes 4194320 | tf_op jit(solution)/shard_map/all_gather | solution.py:29
  432.8 142.9 %all-gather.6.cloned.1.call-done = bf16[64,128,1024]{2,1,0:T(8,128)(2,1)} async-done(((bf16[2,128,1024]{2,1,0:T(8,128)(2,1)}), bf16[64,128,1024]{2,1,0:T(8,128)(2,1)}) %all-gather.6.cloned.1.call-update) | async-done | bytes 16777232 | tf_op jit(solution)/shard_map/all_gather | solution.py:34
  575.8 97.6 %while.11 = (s32[]{:T(128)}, bf16[12,128,1024]{2,1,0:T(8,128)(2,1)S(1)}, s32[]{:T(128)}, s32[12]{0:T(128)S(1)}, bf16[64,128,1024]{2,1,0:T(8,128)(2,1)}, /*index=...) while((s32[]{:T(128)}, ...), condition=%wide.region_18.19_spmd, body=%wide.region_17.18_spmd.sunk | while | flops 268828672 | bytes 3408139 | solution.py:41
  581.3 2.5 fusion.100
  589.4 2.5 fusion.100
  597.5 2.5 fusion.100
  605.6 2.5 fusion.100
  613.6 2.5 fusion.100
  629.8 2.5 fusion.100
  646.0 2.5 fusion.100
  662.1 2.5 fusion.100
  (156 shorter events, 111.8 us)
Async XLA Ops:
  7.2 1.0 copy-start.4
  7.2 2.1 copy-start.5
  7.2 46.1 %all-gather.4.cloned.1.call-start = ((), (), s32[]{:S(2)}) async-start(), calls=%async_computation | async-start | bytes 4718592 | tf_op jit(solution)/shard_map/all_gather | solution.py:23
  9.2 423.6 %all-gather.8.cloned.1.call-start = ((), (), s32[]{:S(2)}) async-start(), calls=%async_computation.2 | async-start | bytes 4718592 | tf_op jit(solution)/shard_map/all_gather | solution.py:29
  9.6 372.6 %copy-start.3 = (f32[1024,256]{1,0:T(8,128)}, f32[1024,256]{1,0:T(8,128)S(1)}, u32[]{:S(2)}) copy-start(f32[1024,256]{1,0:T(8,128)S(1)} %bitcast_convert_fusion) | copy-start | bytes 3145732
  63.1 1.9 copy-start
  374.9 9.7 %copy-start.6 = (f32[8,128,128]{1,2,0:T(8,128)}, f32[8,128,128]{1,2,0:T(8,128)S(1)}, u32[]{:S(2)}) copy-start(f32[8,128,128]{1,2,0:T(8,128)S(1)} %custom-call.69) | copy-start | bytes 1572868
  384.7 13.1 %copy-start.7 = (s32[32,12]{0,1:T(8,128)S(1)}, s32[32,12]{0,1:T(8,128)}, u32[]{:S(2)}) copy-start(s32[32,12]{0,1:T(8,128)} %param.11) | copy-start | bytes 4612
  384.7 13.1 %copy-start.8 = (s32[32,12]{0,1:T(8,128)S(1)}, s32[32,12]{0,1:T(8,128)}, u32[]{:S(2)}) copy-start(s32[32,12]{0,1:T(8,128)} %param.10) | copy-start | bytes 4612
  384.7 191.1 %copy-start.2 = (bf16[1,12,128,1024]{3,2,1,0:T(8,128)(2,1)S(1)}, bf16[1,12,128,1024]{3,2,1,0:T(8,128)(2,1)}, u32[]{:S(2)}) copy-start(bf16[1,12,128,1024]{3,2,1,0:T(8,128)(2,1)} %param.9) | copy-start | bytes 9437188
  397.0 178.7 %all-gather.6.cloned.1.call-start = ((), (), s32[]{:S(2)}) async-start(), calls=%async_computation.1 | async-start | bytes 17301504 | tf_op jit(solution)/shard_map/all_gather | solution.py:34
  673.4 1.7 copy-start.1
Sparse Core Ops, SparseCore 0:
  10.4 42.8 all-gather.3
  397.1 35.6 all-gather.7
  436.0 139.6 all-gather.5
where the time goes:
time: 693 us; the launch traced here: 682 us
  other arithmetic  261 us (38%)
  waiting for transfers between devices  222 us (32%)
  matrix products  73.2 us (11%)
  local copies, waits for them, and re-layouts  53.5 us (8%)
  loops' own time  52.9 us (8%)
  between operations  19.3 us (3%)
    another operation x30, other arithmetic, local(): factor = jnp.linalg.cholesky(diag_full)  173 us
    all_gather x1, waiting for transfers between devices, local(): slices = lax.all_gather(panel_factor, 'col', axis=0, tiled=True)  143 us
    another operation x3, other arithmetic, local(): lax.linalg.triangular_solve(factor, stacked.T, left_side=True, lower=True)  83.6 us
    another operation x1, loops' own time, local(): buffer = lax.fori_loop(0, own_count, own_step, trailing[0])  52.7 us
    all_gather x1, waiting for transfers between devices, local(): diag_full = lax.all_gather(diag_block, 'row', axis=0, tiled=True)  43.7 us
    all_gather x1, waiting for transfers between devices, local(): whole_tiles = lax.all_gather(panel_factor, 'row', axis=1, tiled=True)  34.2 us
    dot_general x12, matrix products, slot_product(): lax.dot_general(left_slice, right_tile, (((1,), (1,)), ((), ())), preferr...  30.3 us
    another operation x14, matrix products, local(): factor = jnp.linalg.cholesky(diag_full)  23.1 us
  transfers between devices with their start and end apart: 3, of which 3 were waited for; matrix products, arithmetic and copies ran while one was open for 0% of the time, Pallas kernels for 0%

commit v1 on v0

--- a/solution.py
+++ b/solution.py
@@ -2,6 +2,34 @@
 import jax.numpy as jnp
 from jax import lax
 from jax.sharding import PartitionSpec as P
+
+
+def raise_the_sample(mesh_name, w_in, on_dim):
+    e_now, h_now, v_next = (lax.axis_size(mesh_name), lax.axis_index(mesh_name), w_in.shape[on_dim])
+    queue = []
+    for it, i0 in enumerate(w_in.shape):
+        queue.append(i0 * e_now if it == on_dim else i0)
+    mat_out = lax.dynamic_update_slice_in_dim(
+        jnp.zeros(queue, w_in.dtype), w_in, h_now * v_next, axis=on_dim
+    )
+    then = taken_in = w_in
+    for w in range(1, e_now // 2 + 1):
+        samples = []
+        for it in range(e_now):
+            samples.append((it, (it + 1) % e_now))
+        then = lax.ppermute(then, mesh_name, samples)
+        mat_out = lax.dynamic_update_slice_in_dim(
+            mat_out, then, (h_now - w) % e_now * v_next, axis=on_dim
+        )
+        if 2 * w < e_now:
+            shelf = []
+            for it in range(e_now):
+                shelf.append((it, (it - 1) % e_now))
+            taken_in = lax.ppermute(taken_in, mesh_name, shelf)
+            mat_out = lax.dynamic_update_slice_in_dim(
+                mat_out, taken_in, (h_now + w) % e_now * v_next, axis=on_dim
+            )
+    return mat_out
 
 
 def slot_product(slices, left_ids, source_tiles, col_ids, position):
@@ -20,7 +48,7 @@
 
 
 def local(diag_block, panel, trailing, slot_rows, slot_cols):
-    diag_full = lax.all_gather(diag_block, "row", axis=0, tiled=True)
+    diag_full = raise_the_sample("row", diag_block, 0)
     factor = jnp.linalg.cholesky(diag_full)
     tile_count, row_count, tile_width = panel.shape
     stacked = panel.astype(jnp.float32).reshape(tile_count * row_count, tile_width)

time: 693 us -> 702 us (1.013)
  waiting for transfers between devices: 222 us -> 192 us
  local copies, waits for them, and re-layouts: 53.5 us -> 76.8 us
  starting transfers between devices: 0.12 us -> 13.2 us
    all_gather x1 -> x0, waiting for transfers between devices: 43.7 us -> none  [local(): diag_full = lax.all_gather(diag_block, 'row', axis=0, tiled=True)]
    dynamic_update_slice x0 -> x9, local copies, waits for them, and re-layouts: none -> 16.5 us  [the longest x5 12 us: raise_the_sample(): lax.dynamic_update_slice_in_dim(mat_out, then, (h_now - w) % e_now * v_ne...]
    ppermute x0 -> x7, starting transfers between devices: none -> 13.1 us  [the longest x4 7.98 us: raise_the_sample(): then = lax.ppermute(then, mesh_name, samples)]
    ppermute x0 -> x7, waiting for transfers between devices: none -> 10.2 us  [the longest x4 9.89 us: raise_the_sample(): then = lax.ppermute(then, mesh_name, samples)]
    another operation x24 -> x40, local copies, waits for them, and re-layouts: 22.8 us -> 28.5 us
  transfers between devices with their start and end apart: 3 -> 9, of which waited for: 3 -> 5; matrix products, arithmetic and copies ran while one was open for 0% -> 2% of each run, Pallas kernels for 0% -> 0%
where the time goes in v1:
time: 702 us; the launch traced here: 690 us
  other arithmetic  257 us (37%)
  waiting for transfers between devices  192 us (27%)
  matrix products  77.6 us (11%)
  local copies, waits for them, and re-layouts  76.8 us (11%)
  loops' own time  52.8 us (8%)
  between operations  19.7 us (3%)
  starting transfers between devices  13.2 us (2%)
    another operation x30, other arithmetic, local(): factor = jnp.linalg.cholesky(diag_full)  168 us
    all_gather x1, waiting for transfers between devices, local(): slices = lax.all_gather(panel_factor, 'col', axis=0, tiled=True)  143 us
    another operation x3, other arithmetic, local(): lax.linalg.triangular_solve(factor, stacked.T, left_side=True, lower=True)  84.4 us
    another operation x1, loops' own time, local(): buffer = lax.fori_loop(0, own_count, own_step, trailing[0])  52.7 us
    all_gather x1, waiting for transfers between devices, local(): whole_tiles = lax.all_gather(panel_factor, 'row', axis=1, tiled=True)  38.3 us
    dot_general x12, matrix products, slot_product(): lax.dot_general(left_slice, right_tile, (((1,), (1,)), ((), ())), preferr...  30.3 us
    another operation x40, local copies, waits for them, and re-layouts  28.5 us
    another operation x14, matrix products, local(): factor = jnp.linalg.cholesky(diag_full)  26.1 us
  transfers between devices with their start and end apart: 9, of which 5 were waited for; matrix products, arithmetic and copies ran while one was open for 2% of the time, Pallas kernels for 0%

profile of v1, /device:TPU:1, one launch (start us, length us, event | category | flops | bytes accessed | tf_op | source)
XLA Modules:
  0.0 689.7 jit_solution(12529706108527238729)
XLA Ops:
  8.4 2.7 collective-permute-start
  11.7 5.5 collective-permute-done
  21.5 4.3 collective-permute-done.2
  25.8 2.6 collective-permute-start.4
  32.1 3.0 collective-permute-start.5
  45.7 5.3 copy.56
  51.0 4.4 fusion.18
  57.4 11.7 %cholesky.222 = f32[128,128]{1,0:T(8,128)S(1)} custom-call(f32[128,128]{1,0:T(8,128)S(1)} %cholesky.577), custom_call_target="Cholesky" | custom-call | tf_op jit(solution)/shard_map/jit(cholesky)/cholesky | solution.py:52
  69.2 9.8 %custom-call.62 = f32[1,128,128]{1,2,0:T(8,128)S(1)} custom-call(f32[1,128,128]{2,1,0:T(8,128)S(1)} %get-tuple-element.121), custom_call_target="InvertDiagBlocksLowerTriangular" | custom-call | tf_op jit(solution)/shard_map/jit(cholesky)/cholesky | solution.py:52
  82.4 11.7 %cholesky.243 = f32[128,128]{1,0:T(8,128)S(1)} custom-call(f32[128,128]{1,0:T(8,128)S(1)} %cholesky.581), custom_call_target="Cholesky" | custom-call | tf_op jit(solution)/shard_map/jit(cholesky)/cholesky | solution.py:52
  94.7 9.8 %custom-call.63 = f32[1,128,128]{1,2,0:T(8,128)S(1)} custom-call(f32[1,128,128]{2,1,0:T(8,128)S(1)} %get-tuple-element.119), custom_call_target="InvertDiagBlocksLowerTriangular" | custom-call | tf_op jit(solution)/shard_map/jit(cholesky)/cholesky | solution.py:52
  110.0 11.7 %cholesky.466 = f32[128,128]{1,0:T(8,128)S(1)} custom-call(f32[128,128]{1,0:T(8,128)S(1)} %cholesky.586), custom_call_target="Cholesky" | custom-call | tf_op jit(solution)/shard_map/jit(cholesky)/cholesky | solution.py:52
  122.5 9.8 %custom-call.64 = f32[1,128,128]{1,2,0:T(8,128)S(1)} custom-call(f32[1,128,128]{2,1,0:T(8,128)S(1)} %get-tuple-element.117), custom_call_target="InvertDiagBlocksLowerTriangular" | custom-call | tf_op jit(solution)/shard_map/jit(cholesky)/cholesky | solution.py:52
  133.6 3.3 slice_subtract_fusion.2
  136.9 11.7 %cholesky.485 = f32[128,128]{1,0:T(8,128)S(1)} custom-call(f32[128,128]{1,0:T(8,128)S(1)} %cholesky.591), custom_call_target="Cholesky" | custom-call | tf_op jit(solution)/shard_map/jit(cholesky)/cholesky | solution.py:52
  149.4 9.8 %custom-call.65 = f32[1,128,128]{1,2,0:T(8,128)S(1)} custom-call(f32[1,128,128]{2,1,0:T(8,128)S(1)} %get-tuple-element.115), custom_call_target="InvertDiagBlocksLowerTriangular" | custom-call | tf_op jit(solution)/shard_map/jit(cholesky)/cholesky | solution.py:52
  160.3 3.2 slice_subtract_fusion.3
  163.5 11.9 %cholesky.504 = f32[128,128]{1,0:T(8,128)S(1)} custom-call(f32[128,128]{1,0:T(8,128)S(1)} %cholesky.596), custom_call_target="Cholesky" | custom-call | tf_op jit(solution)/shard_map/jit(cholesky)/cholesky | solution.py:52
  176.1 9.8 %custom-call.66 = f32[1,128,128]{1,2,0:T(8,128)S(1)} custom-call(f32[1,128,128]{2,1,0:T(8,128)S(1)} %get-tuple-element.113), custom_call_target="InvertDiagBlocksLowerTriangular" | custom-call | tf_op jit(solution)/shard_map/jit(cholesky)/cholesky | solution.py:52
  187.1 3.1 slice_subtract_fusion.4
  190.2 11.7 %cholesky.524 = f32[128,128]{1,0:T(8,128)S(1)} custom-call(f32[128,128]{1,0:T(8,128)S(1)} %cholesky.601), custom_call_target="Cholesky" | custom-call | tf_op jit(solution)/shard_map/jit(cholesky)/cholesky | solution.py:52
  202.7 9.8 %custom-call.67 = f32[1,128,128]{1,2,0:T(8,128)S(1)} custom-call(f32[1,128,128]{2,1,0:T(8,128)S(1)} %get-tuple-element.111), custom_call_target="InvertDiagBlocksLowerTriangular" | custom-call | tf_op jit(solution)/shard_map/jit(cholesky)/cholesky | solution.py:52
  213.5 3.1 slice_subtract_fusion.5
  216.5 11.7 %cholesky.544 = f32[128,128]{1,0:T(8,128)S(1)} custom-call(f32[128,128]{1,0:T(8,128)S(1)} %cholesky.606), custom_call_target="Cholesky" | custom-call | tf_op jit(solution)/shard_map/jit(cholesky)/cholesky | solution.py:52
  229.0 9.8 %custom-call.68 = f32[1,128,128]{1,2,0:T(8,128)S(1)} custom-call(f32[1,128,128]{2,1,0:T(8,128)S(1)} %get-tuple-element.109), custom_call_target="InvertDiagBlocksLowerTriangular" | custom-call | tf_op jit(solution)/shard_map/jit(cholesky)/cholesky | solution.py:52
  241.9 11.7 %cholesky.562 = f32[128,128]{1,0:T(8,128)S(1)} custom-call(f32[128,128]{1,0:T(8,128)S(1)} %slice_subtract_fusion.6), custom_call_target="Cholesky" | custom-call | tf_op jit(solution)/shard_map/jit(cholesky)/cholesky | solution.py:52
  263.9 4.8 select_select_fusion
  268.8 28.6 %while.12 = (s32[]{:T(128)}, f32[1024,1024]{0,1:T(8,128)}, s32[8,2]{0,1:T(2,128)S(1)}, f32[8,128,128]{2,1,0:T(8,128)}, s32[]{:T(128)}) while((s32[]{:T(128)}, f32[1024,1024]{0,1:T(8,128)}, s32[8,2]{0,1:T(2,128)S(1)}, f32[8,128,128]{2,1,0:T(8,128)}, s32[]{:T(128)}) %tuple.69), condition=%wide.while_cond, body=%wide.while_body.sunk | while | flops 2 | bytes 393329 | solution.py:55
  297.4 79.5 %custom-call.69 = f32[8,128,128]{1,2,0:T(8,128)S(1)} custom-call(f32[8,128,128]{2,1,0:T(8,128)} %get-tuple-element.48), custom_call_target="InvertDiagBlocksLowerTriangular" | custom-call | tf_op jit(solution)/shard_map/triangular_solve | solution.py:55
  402.1 38.3 %all-gather.5.cloned.1.call-done = bf16[2,1024,1024]{2,1,0:T(8,128)(2,1)} async-done(((bf16[2,128,1024]{2,1,0:T(8,128)(2,1)}), bf16[2,1024,1024]{2,1,0:T(8,128)(2,1)}) %all-gather.5.cloned.1.call-update) | async-done | bytes 4194320 | tf_op jit(solution)/shard_map/all_gather | solution.py:57
  440.5 142.9 %all-gather.3.cloned.1.call-done = bf16[64,128,1024]{2,1,0:T(8,128)(2,1)} async-done(((bf16[2,128,1024]{2,1,0:T(8,128)(2,1)}), bf16[64,128,1024]{2,1,0:T(8,128)(2,1)}) %all-gather.3.cloned.1.call-update) | async-done | bytes 16777232 | tf_op jit(solution)/shard_map/all_gather | solution.py:62
  583.4 97.6 %while.11 = (s32[]{:T(128)}, bf16[12,128,1024]{2,1,0:T(8,128)(2,1)S(1)}, s32[]{:T(128)}, s32[12]{0:T(128)S(1)}, bf16[64,128,1024]{2,1,0:T(8,128)(2,1)}, /*index=...) while((s32[]{:T(128)}, ...), condition=%wide.region_18.19_spmd, body=%wide.region_17.18_spmd.sunk | while | flops 268828672 | bytes 3408139 | solution.py:69
  (213 shorter events, 148.5 us)
Async XLA Ops:
  7.2 1.0 copy-start.5
  7.2 21.3 %copy-start.6 = (bf16[2,128,1024]{2,1,0:T(8,128)(2,1)S(1)}, bf16[2,128,1024]{2,1,0:T(8,128)(2,1)}, u32[]{:S(2)}) copy-start(bf16[2,128,1024]{2,1,0:T(8,128)(2,1)} %param.8) | copy-start | bytes 1572868
  7.2 433.3 %all-gather.5.cloned.1.call-start = ((), (), s32[]{:S(2)}) async-start(), calls=%async_computation.1 | async-start | bytes 4718592 | tf_op jit(solution)/shard_map/all_gather | solution.py:57
  8.4 8.8 %collective-permute-start = (f32[128,1024]{0,1:T(8,128)S(1)}, f32[128,1024]{0,1:T(8,128)S(1)}, u32[]{:S(2)}, u32[]{:S(2)}) collective-permute-start(f32[128,1024]{0,1:T(8,128)S(1)} %copy.53), channel_id=1, source_target_pairs={{0,32},{32,64},{64,96},{96,128},{128,160},{160,192},{192,224},{224... | collective-permute-start | bytes 1572872 | tf_op jit(solution)/shard_map/ppermute | solution.py:20
  11.1 8.9 %collective-permute-start.1 = (f32[128,1024]{0,1:T(8,128)S(1)}, f32[128,1024]{0,1:T(8,128)S(1)}, u32[]{:S(2)}, u32[]{:S(2)}) collective-permute-start(f32[128,1024]{0,1:T(8,128)S(1)} %copy.53), channel_id=1, source_target_pairs={{0,224},{32,0},{64,32},{96,64},{128,96},{160,128},{192,160},{224,1... | collective-permute-start | bytes 1572872 | tf_op jit(solution)/shard_map/ppermute | solution.py:28
  17.2 13.9 %copy-start.7 = (f32[128,1024]{0,1:T(8,128)}, f32[128,1024]{0,1:T(8,128)S(1)}, u32[]{:S(2)}) copy-start(f32[128,1024]{0,1:T(8,128)S(1)} %collective-permute-done) | copy-start | bytes 1572868
  17.2 8.6 %collective-permute-start.2 = (f32[128,1024]{0,1:T(8,128)S(1)}, f32[128,1024]{0,1:T(8,128)}, u32[]{:S(2)}, u32[]{:S(2)}) collective-permute-start(f32[128,1024]{0,1:T(8,128)S(1)} %collective-permute-done), channel_id=1, source_target_pairs={{0,32},{32,64},{64,96},{96,128},{128,160},{160,192},{192,224},{224... | collective-permute-start | bytes 1572872 | tf_op jit(solution)/shard_map/ppermute | solution.py:20
  20.0 12.1 %collective-permute-start.3 = (f32[128,1024]{0,1:T(8,128)S(1)}, f32[128,1024]{0,1:T(8,128)}, u32[]{:S(2)}, u32[]{:S(2)}) collective-permute-start(f32[128,1024]{0,1:T(8,128)S(1)} %collective-permute-done.1), channel_id=1, source_target_pairs={{0,224},{32,0},{64,32},{96,64},{128,96},{160,128},{192,160},{224,1... | collective-permute-start | bytes 1572872 | tf_op jit(solution)/shard_map/ppermute | solution.py:28
  25.8 11.3 %collective-permute-start.4 = (f32[128,1024]{0,1:T(8,128)}, f32[128,1024]{0,1:T(8,128)}, u32[]{:S(2)}, u32[]{:S(2)}) collective-permute-start(f32[128,1024]{0,1:T(8,128)} %collective-permute-done.2), channel_id=1, source_target_pairs={{0,32},{32,64},{64,96},{96,128},{128,160},{160,192},{192,224},{224... | collective-permute-start | bytes 1572872 | tf_op jit(solution)/shard_map/ppermute | solution.py:20
  32.1 352.5 %copy-start.4 = (f32[1024,256]{1,0:T(8,128)}, f32[1024,256]{1,0:T(8,128)S(1)}, u32[]{:S(2)}) copy-start(f32[1024,256]{1,0:T(8,128)S(1)} %bitcast_convert_fusion) | copy-start | bytes 3145732
  32.1 11.8 %collective-permute-start.5 = (f32[128,1024]{0,1:T(8,128)}, f32[128,1024]{0,1:T(8,128)S(1)}, u32[]{:S(2)}, u32[]{:S(2)}) collective-permute-start(f32[128,1024]{0,1:T(8,128)} %collective-permute-done.3), channel_id=1, source_target_pairs={{0,224},{32,0},{64,32},{96,64},{128,96},{160,128},{192,160},{224,1... | collective-permute-start | bytes 1572872 | tf_op jit(solution)/shard_map/ppermute | solution.py:28
  37.1 7.7 %collective-permute-start.6 = (f32[128,1024]{0,1:T(8,128)}, f32[128,1024]{0,1:T(8,128)S(1)}, u32[]{:S(2)}, u32[]{:S(2)}) collective-permute-start(f32[128,1024]{0,1:T(8,128)} %collective-permute-done.4), channel_id=1, source_target_pairs={{0,32},{32,64},{64,96},{96,128},{128,160},{160,192},{192,224},{224... | collective-permute-start | bytes 1572872 | tf_op jit(solution)/shard_map/ppermute | solution.py:20
  55.4 1.9 copy-start.1
  105.6 2.0 copy-start
  377.0 10.2 %copy-start.8 = (f32[8,128,128]{1,2,0:T(8,128)}, f32[8,128,128]{1,2,0:T(8,128)S(1)}, u32[]{:S(2)}) copy-start(f32[8,128,128]{1,2,0:T(8,128)S(1)} %custom-call.69) | copy-start | bytes 1572868
  387.2 14.0 %copy-start.9 = (s32[32,12]{0,1:T(8,128)S(1)}, s32[32,12]{0,1:T(8,128)}, u32[]{:S(2)}) copy-start(s32[32,12]{0,1:T(8,128)} %param.11) | copy-start | bytes 4612
  387.3 14.0 %copy-start.10 = (s32[32,12]{0,1:T(8,128)S(1)}, s32[32,12]{0,1:T(8,128)}, u32[]{:S(2)}) copy-start(s32[32,12]{0,1:T(8,128)} %param.10) | copy-start | bytes 4612
  387.3 196.1 %copy-start.3 = (bf16[1,12,128,1024]{3,2,1,0:T(8,128)(2,1)S(1)}, bf16[1,12,128,1024]{3,2,1,0:T(8,128)(2,1)}, u32[]{:S(2)}) copy-start(bf16[1,12,128,1024]{3,2,1,0:T(8,128)(2,1)} %param.9) | copy-start | bytes 9437188
  400.5 182.9 %all-gather.3.cloned.1.call-start = ((), (), s32[]{:S(2)}) async-start(), calls=%async_computation | async-start | bytes 17301504 | tf_op jit(solution)/shard_map/all_gather | solution.py:62
  681.0 1.7 copy-start.2
Sparse Core Ops, SparseCore 0:
  400.6 39.8 all-gather.4
  443.6 139.6 all-gather.2
